TPU v7x, 32 devices: a whole 2x2x4 slice. The times are simulated.
32 devices in a mesh: dp: 4 (over y, core), row: 2 (over x), col: 4 (over z).
Axes of the slice: x: 2, y: 2, z: 4, core: 2. Of those that a mesh axis runs over, the one named last changes fastest.
Arguments:
- tokens: bfloat16 [12288, 768], P(('dp', 'col'), 'row'), may hold values from -6 to 6
- cotangent: bfloat16 [12288, 768], P(('dp', 'col'), 'row'), may hold values from -6 to 6
- timestep: int32 [4], P('dp'), may hold values from 0 to 999
- piece_starts: int32 [4, 4], P('dp'), may hold values from 0 to 2816, as said below
- w_mod: bfloat16 [128, 6, 768], P(None, None, 'row'), may hold values from -0.5 to 0.5
- b_mod: float32 [6, 768], P(None, 'row'), may hold values from -3 to 3
- gain_attn: float32 [768], P('row'), may hold values from 0.5 to 1.5
- w_qkv: bfloat16 [2304, 768], P('col', 'row'), may hold values from -0.21875 to 0.21875
- w_out: bfloat16 [768, 768], P('col', 'row'), may hold values from -0.875 to 0.875
- gain_mlp: float32 [768], P('row'), may hold values from 0.5 to 1.5
- w_up: bfloat16 [768, 3072], P('row', 'col'), may hold values from -0.21875 to 0.21875
- b_up: bfloat16 [3072], P('col'), may hold values from -3 to 3
- w_down: bfloat16 [3072, 768], P('col', 'row'), may hold values from -0.109375 to 0.109375
- b_down: float32 [768], P('row'), may hold values from -3 to 3
Outputs:
- block_out: bfloat16 [12288, 768], P(('dp', 'col'), 'row')
- d_tokens: float32 [12288, 768], P(('dp', 'col'), 'row')
- d_mod_w: float32 [128, 6, 768], P(None, None, 'row')
- d_mod_b: float32 [6, 768], P(None, 'row')
- d_gain_attn: float32 [768], P('row')
- d_qkv: float32 [2304, 768], P('col', 'row')
- d_out_proj: float32 [768, 768], P('col', 'row')
- d_gain_mlp: float32 [768], P('row')
- d_up: float32 [768, 3072], P('row', 'col')
- d_up_bias: float32 [3072], P('col')
- d_down: float32 [3072, 768], P('col', 'row')
- d_down_bias: float32 [768], P('row')
Inputs may be any that keep to these rules, and one draw needn't show every extreme that they name: `piece_starts`: in every sequence the 4 pieces of 256 tokens rise, do not intersect and lie inside the sequence; the first opens the sequence and the last closes it.
All inputs are finite; a program needn't handle non-finite values.
Results may differ from a plain program's by a relative error of at most 0.014.
The roundings to bfloat16 on the way count: a program that leaves them out, or rounds other values in their place, can miss the bound.
Values may be sent and summed in bfloat16 or wider, within the bound.
No kernel may reach another device: no remote copies, remote signals or barrier semaphores. Data moves between devices by JAX's collectives and lax.ppermute only.
A program may use at most 192 MiB of HBM per device.

v0:
```python
import math
import jax
import jax.numpy as jnp
from jax import lax
from jax.sharding import PartitionSpec as P

D = 768
HEAD = 64
COND = 128
PIECE = 256
PIECES = 4
precise = lax.Precision.HIGHEST
epsilon = 1e-05


def embed_time(time_step):
    half_size = COND // 2
    frequency = jnp.exp(-math.log(10000.0) * jnp.arange(half_size, dtype=jnp.float32) / half_size)
    angles = time_step * frequency
    return jax.nn.silu(jnp.concatenate([jnp.cos(angles), jnp.sin(angles)]))


def rotate(vectors, places):
    half_size = HEAD // 2
    frequency = jnp.exp(-math.log(10000.0) * jnp.arange(half_size, dtype=jnp.float32) / half_size)
    angles = places.astype(jnp.float32)[:, None] * frequency[None, :]
    cosine = jnp.cos(angles)[:, None, :]
    sine_part = jnp.sin(angles)[:, None, :]
    first_half = vectors[..., :half_size]
    second_half = vectors[..., half_size:]
    return jnp.concatenate(
        [
            first_half * cosine - second_half * sine_part,
            second_half * cosine + first_half * sine_part,
        ],
        -1,
    )


def piece_ids(places, starts):
    inside = (places[:, None] >= starts[None, :]) & (places[:, None] < starts[None, :] + PIECE)
    labels = jnp.arange(1, PIECES + 1, dtype=jnp.int32)[None, :]
    return jnp.sum(jnp.where(inside, labels, 0), axis=1) - 1


def visible(query_places, seq_len, starts):
    key_places = jnp.arange(seq_len, dtype=jnp.int32)
    query_piece = piece_ids(query_places, starts)
    key_piece = piece_ids(key_places, starts)
    return (key_places[None, :] <= query_places[:, None]) | (
        query_piece[:, None] == key_piece[None, :]
    ) & (query_piece[:, None] >= 0)


def into_heads(activation, weight, contract):
    gathered = lax.all_gather(activation, "col", axis=0, tiled=True)
    share_rows = gathered.shape[0] // lax.axis_size("row")

    def partial_product(start_row, row_count):
        return lax.dot_general(
            gathered, weight, (((1,), (contract,)), ((), ())), preferred_element_type=jnp.float32
        )

    return (
        lax.psum_scatter(
            partial_product(jnp.int32(0), share_rows * lax.axis_size("row")),
            "row",
            scatter_dimension=0,
            tiled=True,
        ),
        gathered,
    )


def into_stream(activation, weight, contract):
    gathered = lax.all_gather(activation, "row", axis=0, tiled=True)
    share_rows = gathered.shape[0] // lax.axis_size("col")

    def partial_product(start_row, row_count):
        return lax.dot_general(
            gathered, weight, (((1,), (contract,)), ((), ())), preferred_element_type=jnp.float32
        )

    return (
        lax.psum_scatter(
            partial_product(jnp.int32(0), share_rows * lax.axis_size("col")),
            "col",
            scatter_dimension=0,
            tiled=True,
        ),
        gathered,
    )


def weight_grad(first_operand, second_operand):
    return lax.dot_general(
        first_operand, second_operand, (((0,), (0,)), ((), ())), preferred_element_type=jnp.float32
    )


def row_totals(first_sum, second_sum):
    return lax.psum((first_sum, second_sum), "row")


def norm_forward(values, gain_vec, shift_vec, scale_vec, totals):
    row_total, row_square = totals(jnp.sum(values, -1), jnp.sum(values * values, -1))
    row_mean = row_total / D
    inv_std = lax.rsqrt(row_square / D - row_mean * row_mean + epsilon)
    normed = (values - row_mean[:, None]) * inv_std[:, None]
    return (
        normed,
        inv_std,
        (normed * gain_vec * (1.0 + scale_vec) + shift_vec).astype(jnp.bfloat16),
    )


def norm_backward(upstream, normed, inv_std, gain_vec, scale_vec, totals):
    d_shift = jnp.sum(upstream, 0)
    d_scale = jnp.sum(upstream * normed * gain_vec, 0)
    d_gain = jnp.sum(upstream * normed * (1.0 + scale_vec), 0)
    d_normed = upstream * gain_vec * (1.0 + scale_vec)
    mean_grad, mean_proj = totals(jnp.sum(d_normed, -1), jnp.sum(d_normed * normed, -1))
    d_values = inv_std[:, None] * (
        d_normed - mean_grad[:, None] / D - normed * mean_proj[:, None] / D
    )
    return (d_values, d_gain, d_shift, d_scale)


def attend(query_head, key_head, value_head, allowed):
    scores = lax.dot_general(
        query_head, key_head, (((1,), (1,)), ((), ())), preferred_element_type=jnp.float32
    ) * HEAD ** (-0.5)
    scores = jnp.where(allowed, scores, -1e30)
    row_max = jnp.max(scores, -1, keepdims=True)
    weights_raw = jnp.exp(scores - row_max)
    row_sum = jnp.sum(weights_raw, -1, keepdims=True)
    probabilities = (weights_raw / row_sum).astype(jnp.bfloat16)
    mixed_head = jnp.dot(probabilities, value_head, preferred_element_type=jnp.float32)
    return (mixed_head, (row_max + jnp.log(row_sum))[:, 0])


def attend_back(query_head, key_head, value_head, d_mixed_head, log_sum, allowed):
    scores = lax.dot_general(
        query_head, key_head, (((1,), (1,)), ((), ())), preferred_element_type=jnp.float32
    ) * HEAD ** (-0.5)
    probabilities = jnp.where(allowed, jnp.exp(scores - log_sum[:, None]), 0.0)
    d_prob = lax.dot_general(
        d_mixed_head, value_head, (((1,), (1,)), ((), ())), preferred_element_type=jnp.float32
    )
    d_scores = (
        probabilities * (d_prob - jnp.sum(probabilities * d_prob, -1, keepdims=True))
    ).astype(jnp.bfloat16)
    d_query = jnp.dot(d_scores, key_head, preferred_element_type=jnp.float32) * HEAD ** (-0.5)
    d_key = weight_grad(d_scores, query_head) * HEAD ** (-0.5)
    d_value = weight_grad(probabilities.astype(jnp.bfloat16), d_mixed_head)
    return (d_query, d_key, d_value)


def rotate_pair(projected, places):
    return jax.vjp(
        lambda first_in, second_in: (rotate(first_in, places), rotate(second_in, places)),
        projected[:, :, 0],
        projected[:, :, 1],
    )


def attention_forward(queries, key_value_all, allowed):
    heads_query = queries.transpose(1, 0, 2)
    heads_key = key_value_all[:, :, 0].transpose(1, 0, 2)
    heads_value = key_value_all[:, :, 1].transpose(1, 0, 2)
    mixed, log_sum = lax.map(
        lambda operands: attend(operands[0], operands[1], operands[2], allowed),
        (heads_query, heads_key, heads_value),
    )
    mixed = (
        mixed.transpose(1, 0, 2)
        .reshape(queries.shape[0], queries.shape[1] * HEAD)
        .astype(jnp.bfloat16)
    )
    return (mixed, log_sum, (heads_query, heads_key, heads_value))


def attention_backward(saved, d_mixed, log_sum, allowed):
    heads_query, heads_key, heads_value = saved
    head_count = heads_query.shape[0]
    query_rows = heads_query.shape[1]
    seq_len = heads_key.shape[1]
    d_mixed_heads = (
        d_mixed.astype(jnp.bfloat16).reshape(query_rows, head_count, HEAD).transpose(1, 0, 2)
    )
    d_query, d_key, d_value = lax.map(
        lambda operands: attend_back(
            operands[0], operands[1], operands[2], operands[3], operands[4], allowed
        ),
        (heads_query, heads_key, heads_value, d_mixed_heads, log_sum),
    )
    d_key_value = jnp.stack([d_key.transpose(1, 0, 2), d_value.transpose(1, 0, 2)], 2).reshape(
        seq_len, head_count * 2 * HEAD
    )
    return (d_query.transpose(1, 0, 2), d_key_value)


def small_stack(
    d_shift_attn,
    d_scale_attn,
    d_gate_attn,
    d_shift_mlp,
    d_scale_mlp,
    d_gate_mlp,
    d_gain_attn,
    d_gain_mlp,
    d_down_bias,
):
    return jnp.stack(
        [
            d_shift_attn,
            d_scale_attn,
            d_gate_attn,
            d_shift_mlp,
            d_scale_mlp,
            d_gate_mlp,
            d_gain_attn,
            d_gain_mlp,
            d_down_bias,
        ],
        0,
    )


def blocked_layer(
    tokens,
    cotangent,
    modulation,
    starts,
    gain_attn,
    w_qkv,
    w_out,
    gain_mlp,
    w_up,
    b_up,
    w_down,
    b_down,
):
    residual = tokens.astype(jnp.float32)
    shift_attn, scale_attn, gate_attn = (modulation[0], modulation[1], modulation[2])
    shift_mlp, scale_mlp, gate_mlp = (modulation[3], modulation[4], modulation[5])
    normed_one, inv_std_one, normed_in = norm_forward(
        residual, gain_attn, shift_attn, scale_attn, row_totals
    )
    projected, normed_in_all = into_heads(normed_in, w_qkv, 1)
    query_rows = projected.shape[0]
    heads_local = projected.shape[1] // (3 * HEAD)
    projected = projected.reshape(query_rows, heads_local, 3, HEAD)
    seq_len = query_rows * lax.axis_size("row")
    query_places = lax.axis_index("row") * query_rows + jnp.arange(query_rows, dtype=jnp.int32)
    rotated, rotate_back = rotate_pair(projected, query_places)
    queries = rotated[0].astype(jnp.bfloat16)
    key_value = jnp.stack(
        [rotated[1].astype(jnp.bfloat16), projected[:, :, 2].astype(jnp.bfloat16)], 2
    ).reshape(query_rows, heads_local * 2 * HEAD)
    key_value_all = lax.all_gather(key_value, "row", axis=0, tiled=True).reshape(
        seq_len, heads_local, 2, HEAD
    )
    allowed = visible(query_places, seq_len, starts)
    mixed, log_sum, saved = attention_forward(queries, key_value_all, allowed)
    attended, mixed_all = into_stream(mixed, w_out, 0)
    middle = residual + gate_attn * attended
    normed_two, inv_std_two, normed_mid = norm_forward(
        middle, gain_mlp, shift_mlp, scale_mlp, row_totals
    )
    hidden, normed_mid_all = into_heads(normed_mid, w_up, 0)
    hidden = hidden + b_up.astype(jnp.float32)
    active_full, gelu_back = jax.vjp(lambda inner: jax.nn.gelu(inner, approximate=True), hidden)
    active = active_full.astype(jnp.bfloat16)
    branch, active_all = into_stream(active, w_down, 0)
    branch = branch + b_down
    block_out = (middle + gate_mlp * branch).astype(jnp.bfloat16)
    upstream = cotangent.astype(jnp.float32)
    d_gate_mlp = jnp.sum(upstream * branch, 0)
    d_branch = (upstream * gate_mlp).astype(jnp.bfloat16)
    d_down_bias = jnp.sum(d_branch.astype(jnp.float32), 0)
    d_active, d_branch_all = into_heads(d_branch, w_down, 1)
    d_down = weight_grad(active_all, d_branch_all)
    d_hidden = gelu_back(d_active)[0].astype(jnp.bfloat16)
    d_up_bias = jnp.sum(d_hidden.astype(jnp.float32), 0)
    d_normed_mid, d_hidden_all = into_stream(d_hidden, w_up, 1)
    d_up = weight_grad(normed_mid_all, d_hidden_all)
    d_middle, d_gain_mlp, d_shift_mlp, d_scale_mlp = norm_backward(
        d_normed_mid, normed_two, inv_std_two, gain_mlp, scale_mlp, row_totals
    )
    d_middle = d_middle + upstream
    d_gate_attn = jnp.sum(d_middle * attended, 0)
    d_attended = (d_middle * gate_attn).astype(jnp.bfloat16)
    d_mixed, d_attended_all = into_heads(d_attended, w_out, 1)
    d_out_proj = weight_grad(mixed_all, d_attended_all)
    d_query, d_key_value = attention_backward(saved, d_mixed, log_sum, allowed)
    d_key_value = (
        lax.psum_scatter(d_key_value.astype(jnp.bfloat16), "row", scatter_dimension=0, tiled=True)
        .astype(jnp.float32)
        .reshape(query_rows, heads_local, 2, HEAD)
    )
    d_query_raw, d_key_raw = rotate_back((d_query, d_key_value[:, :, 0]))
    d_projected = (
        jnp.stack([d_query_raw, d_key_raw, d_key_value[:, :, 1]], 2)
        .reshape(query_rows, heads_local * 3 * HEAD)
        .astype(jnp.bfloat16)
    )
    d_normed_in, d_projected_all = into_stream(d_projected, w_qkv, 0)
    d_qkv = weight_grad(d_projected_all, normed_in_all)
    d_input, d_gain_attn, d_shift_attn, d_scale_attn = norm_backward(
        d_normed_in, normed_one, inv_std_one, gain_attn, scale_attn, row_totals
    )
    d_tokens = d_input + d_middle
    small_rows = small_stack(
        d_shift_attn,
        d_scale_attn,
        d_gate_attn,
        d_shift_mlp,
        d_scale_mlp,
        d_gate_mlp,
        d_gain_attn,
        d_gain_mlp,
        d_down_bias,
    )
    row_here = lax.axis_index("row")
    col_here = lax.axis_index("col")
    row_slots = jnp.where(
        (jnp.arange(lax.axis_size("row"), dtype=jnp.int32) == row_here)[:, None, None],
        small_rows[None],
        0.0,
    )
    col_slots = jnp.where(
        (jnp.arange(lax.axis_size("col"), dtype=jnp.int32) == col_here)[:, None],
        d_up_bias[None],
        0.0,
    )
    row_slots, col_slots = lax.psum((row_slots, col_slots), ("row", "col"))
    small_rows = lax.dynamic_index_in_dim(row_slots, row_here, 0, keepdims=False)
    d_up_bias = lax.dynamic_index_in_dim(col_slots, col_here, 0, keepdims=False)
    return (block_out, d_tokens, d_qkv, d_out_proj, d_up, d_down, small_rows, d_up_bias)


def shards(
    tokens,
    cotangent,
    timestep,
    piece_starts,
    w_mod,
    b_mod,
    gain_attn,
    w_qkv,
    w_out,
    gain_mlp,
    w_up,
    b_up,
    w_down,
    b_down,
):
    condition = embed_time(timestep[0].astype(jnp.float32))
    modulation = (
        jnp.einsum("k,kjd->jd", condition, w_mod.astype(jnp.float32), precision=precise) + b_mod
    )
    starts = piece_starts[0]
    results = blocked_layer(
        tokens,
        cotangent,
        modulation,
        starts,
        gain_attn,
        w_qkv,
        w_out,
        gain_mlp,
        w_up,
        b_up,
        w_down,
        b_down,
    )
    block_out, d_tokens, d_qkv, d_out_proj, d_up, d_down, small_rows, d_up_bias = results
    d_mod_w = condition[:, None, None] * small_rows[:6][None, :, :]
    d_qkv, d_out_proj, d_up, d_down, d_mod_w, small_rows, d_up_bias = lax.psum(
        (d_qkv, d_out_proj, d_up, d_down, d_mod_w, small_rows, d_up_bias), "dp"
    )
    return (
        block_out,
        d_tokens,
        d_mod_w,
        small_rows[:6],
        small_rows[6],
        d_qkv,
        d_out_proj,
        small_rows[7],
        d_up,
        d_up_bias,
        d_down,
        small_rows[8],
    )


def solution(mesh):
    return jax.shard_map(
        shards,
        mesh=mesh,
        in_specs=(
            P(("dp", "col"), "row"),
            P(("dp", "col"), "row"),
            P("dp"),
            P("dp", None),
            P(None, None, "row"),
            P(None, "row"),
            P("row"),
            P("col", "row"),
            P("col", "row"),
            P("row"),
            P("row", "col"),
            P("col"),
            P("col", "row"),
            P("row"),
        ),
        out_specs=(
            P(("dp", "col"), "row"),
            P(("dp", "col"), "row"),
            P(None, None, "row"),
            P(None, "row"),
            P("row"),
            P("col", "row"),
            P("col", "row"),
            P("row"),
            P("row", "col"),
            P("col"),
            P("col", "row"),
            P("row"),
        ),
        check_vma=False,
    )
```

profile of v0, /device:TPU:0, one launch (start us, length us, event | category | flops | bytes accessed | tf_op | source)
XLA Modules:
  0.0 1633.3 jit_solution(5533274232627833205)
XLA Ops:
  19.4 51.9 %all-gather.10.cloned.1.call-done = bf16[3072,384]{1,0:T(8,128)(2,1)} async-done(((bf16[768,384]{1,0:T(8,128)(2,1)}), bf16[3072,384]{1,0:T(8,128)(2,1)}) %all-gather.10.cloned.1.call-update) | async-done | bytes 2359312 | tf_op jit(solution)/shard_map/all_gather | solution.py:56
  79.3 83.1 %reduce-scatter.10.cloned.1.call-done = f32[1536,576]{0,1:T(8,128)} async-done(((f32[3072,576]{0,1:T(8,128)}), f32[1536,576]{0,1:T(8,128)}) %reduce-scatter.10.cloned.1.call-update) | async-done | bytes 3538960 | tf_op jit(solution)/shard_map/reduce_scatter | solution.py:65
  172.0 31.4 %all-gather.12.cloned.1.call-done = bf16[3072,384]{0,1:T(8,128)(2,1)} async-done(((bf16[1536,384]{0,1:T(8,128)(2,1)}), bf16[3072,384]{0,1:T(8,128)(2,1)}) %all-gather.12.cloned.1.call-update) | async-done | bytes 2359312 | tf_op jit(solution)/shard_map/all_gather | solution.py:261
  213.1 93.5 %while.30 = (s32[]{:T(128)}, bf16[3,1536,64]{1,2,0:T(8,128)(2,1)S(1)}, f32[3,1536]{1,0:T(4,128)}, bf16[3,1536,64]{2,1,0:T(8,128)(2,1)}, bf16[3,3072,64]{2,1,0:T(...) while((s32[]{:T(128)}, ...), condition=%wide.region_10.11_spmd.clone.clone, body=%wide.region_7.10_spmd.clone.sunk.clone | while | flops 1264581120 | bytes 59093104 | solution.py:171
  213.1 12.4 fusion.165
  244.3 12.3 fusion.165
  275.5 12.3 fusion.165
  307.6 22.9 %all-gather.14.cloned.1.call-done = bf16[3072,192]{0,1:T(8,128)(2,1)} async-done(((bf16[1536,192]{0,1:T(8,128)(2,1)}), bf16[3072,192]{0,1:T(8,128)(2,1)}) %all-gather.14.cloned.1.call-update) | async-done | bytes 1179664 | tf_op jit(solution)/shard_map/all_gather | solution.py:76
  337.5 82.8 %reduce-scatter.12.cloned.1.call-done = f32[768,384]{1,0:T(8,128)} async-done(((f32[3072,384]{1,0:T(8,128)}), f32[768,384]{1,0:T(8,128)}) %reduce-scatter.12.cloned.1.call-update) | async-done | bytes 1179664 | tf_op jit(solution)/shard_map/reduce_scatter | solution.py:85
  428.4 44.5 %all-gather.20.cloned.1.call-done = bf16[3072,384]{1,0:T(8,128)(2,1)} async-done(((bf16[768,384]{1,0:T(8,128)(2,1)}), bf16[3072,384]{1,0:T(8,128)(2,1)}) %all-gather.20.cloned.1.call-update) | async-done | bytes 2359312 | tf_op jit(solution)/shard_map/all_gather | solution.py:56
  480.9 42.9 %all-gather.16.cloned.1.call-done = bf16[3072,384]{1,0:T(8,128)(2,1)} async-done(((bf16[768,384]{1,0:T(8,128)(2,1)}), bf16[3072,384]{1,0:T(8,128)(2,1)}) %all-gather.16.cloned.1.call-update) | async-done | bytes 2359312 | tf_op jit(solution)/shard_map/all_gather | solution.py:56
  532.6 102.9 %reduce-scatter.18.cloned.1.call-done = f32[1536,768]{1,0:T(8,128)} async-done(((f32[3072,768]{1,0:T(8,128)}), f32[1536,768]{1,0:T(8,128)}) %reduce-scatter.18.cloned.1.call-update) | async-done | bytes 4718608 | tf_op jit(solution)/shard_map/reduce_scatter | solution.py:65
  635.5 113.0 %reduce-scatter.14.cloned.1.call-done = f32[1536,768]{1,0:T(8,128)} async-done(((f32[3072,768]{1,0:T(8,128)}), f32[1536,768]{1,0:T(8,128)}) %reduce-scatter.14.cloned.1.call-update) | async-done | bytes 4718608 | tf_op jit(solution)/shard_map/reduce_scatter | solution.py:65
  757.7 62.0 %all-gather.22.cloned.1.call-done = bf16[3072,768]{1,0:T(8,128)(2,1)} async-done(((bf16[1536,768]{1,0:T(8,128)(2,1)}), bf16[3072,768]{1,0:T(8,128)(2,1)}) %all-gather.22.cloned.1.call-update) | async-done | bytes 4718608 | tf_op jit(solution)/shard_map/all_gather | solution.py:76
  826.8 57.0 %all-gather.18.cloned.1.call-done = bf16[3072,768]{1,0:T(8,128)(2,1)} async-done(((bf16[1536,768]{1,0:T(8,128)(2,1)}), bf16[3072,768]{1,0:T(8,128)(2,1)}) %all-gather.18.cloned.1.call-update) | async-done | bytes 4718608 | tf_op jit(solution)/shard_map/all_gather | solution.py:76
  891.5 79.8 %reduce-scatter.20.cloned.1.call-done = f32[768,384]{1,0:T(8,128)} async-done(((f32[3072,384]{1,0:T(8,128)}), f32[768,384]{1,0:T(8,128)}) %reduce-scatter.20.cloned.1.call-update) | async-done | bytes 1179664 | tf_op jit(solution)/shard_map/reduce_scatter | solution.py:85
  978.9 80.6 %reduce-scatter.16.cloned.1.call-done = f32[768,384]{1,0:T(8,128)} async-done(((f32[3072,384]{1,0:T(8,128)}), f32[768,384]{1,0:T(8,128)}) %reduce-scatter.16.cloned.1.call-update) | async-done | bytes 1179664 | tf_op jit(solution)/shard_map/reduce_scatter | solution.py:85
  1065.0 50.6 %all-gather.24.cloned.1.call-done = bf16[3072,384]{1,0:T(8,128)(2,1)} async-done(((bf16[768,384]{1,0:T(8,128)(2,1)}), bf16[3072,384]{1,0:T(8,128)(2,1)}) %all-gather.24.cloned.1.call-update) | async-done | bytes 2359312 | tf_op jit(solution)/shard_map/all_gather | solution.py:56
  1119.8 33.6 %reduce-scatter.22.cloned.1.call-done = f32[1536,192]{0,1:T(8,128)} async-done(((f32[3072,192]{0,1:T(8,128)}), f32[1536,192]{0,1:T(8,128)}) %reduce-scatter.22.cloned.1.call-update) | async-done | bytes 1179664 | tf_op jit(solution)/shard_map/reduce_scatter | solution.py:65
  1156.0 147.2 %while.31 = (s32[]{:T(128)}, f32[3,1536,64]{1,2,0:T(8,128)}, bf16[3,3072,64]{1,2,0:T(8,128)(2,1)}, bf16[3,3072,64]{1,2,0:T(8,128)(2,1)}, bf16[3,1536,64]{2,1,0:T...) while((s32[]{:T(128)}, f32[3,1536,64]{1,2,0:T(8,128)}, ...), condition=%wide.region_27.28_spmd.clone.clone, body=%wide.region_25.27_spmd.clone.sunk.clone | while | flops 3081533952 | bytes 189987504 | solution.py:191
  1165.9 13.4 multiply_reduce_fusion.10
  1179.3 13.0 multiply_convert_fusion.5
  1215.0 13.4 multiply_reduce_fusion.10
  1228.4 13.0 multiply_convert_fusion.5
  1264.0 13.4 multiply_reduce_fusion.10
  1277.4 13.0 multiply_convert_fusion.5
  1306.7 34.7 %reduce-scatter.24.cloned.1.call-done = bf16[1536,384]{0,1:T(8,128)(2,1)} async-done(((bf16[3072,384]{0,1:T(8,128)(2,1)}), bf16[1536,384]{0,1:T(8,128)(2,1)}) %reduce-scatter.24.cloned.1.call-update) | async-done | bytes 1179664 | tf_op jit(solution)/shard_map/reduce_scatter | solution.py:298
  1345.5 49.4 %all-gather.26.cloned.1.call-done = bf16[3072,576]{0,1:T(8,128)(2,1)} async-done(((bf16[1536,576]{0,1:T(8,128)(2,1)}), bf16[3072,576]{0,1:T(8,128)(2,1)}) %all-gather.26.cloned.1.call-update) | async-done | bytes 3538960 | tf_op jit(solution)/shard_map/all_gather | solution.py:76
  1419.7 67.3 %reduce-scatter.26.cloned.1.call-done = f32[768,384]{1,0:T(8,128)} async-done(((f32[3072,384]{1,0:T(8,128)}), f32[768,384]{1,0:T(8,128)}) %reduce-scatter.26.cloned.1.call-update) | async-done | bytes 1179664 | tf_op jit(solution)/shard_map/reduce_scatter | solution.py:85
  1489.3 37.4 %all-reduce.4 = (f32[2,9,384]{2,1,0:T(8,128)S(1)}, f32[4,768]{1,0:T(4,128)S(1)}) all-reduce(f32[2,9,384]{2,1,0:T(8,128)S(1)} %broadcast_select_fusion, f32[4,768]{1,0:T(4,128)S(1)} %broadcast_select_fusion.1), channel_id=1, replica_groups=mesh['dp'=4,'row'=2,'col'=4] {'row','col'}, use_global_device_ids=true, to_apply=%region_43.44 | all-reduce | flops 9984 | bytes 79872 | tf_op jit(solution)/shard_map/psum | solution.py:337
  1528.0 11.9 all-reduce.5
  1547.6 72.0 %all-reduce.13.cloned.1.call-done = (f32[128,6,384]{2,0,1:T(8,128)}, f32[576,384]{1,0:T(8,128)}, f32[192,384]{1,0:T(8,128)}, f32[384,768]{1,0:T(8,128)}, f32[768,384]{1,0:T(8,128)}) async-done(((f32[128,6,384]{2,0,1:T(8,128)}, f32[576,384]{1,0:T(8,128)}, f32[192,384]{1,0:T(8,128)}, f32[384,768]{1,0:T(8,128)}, f32[768,384]{1,0:T(8,128)}), (f32[128,6,384]{2,0,1:T(8,128)}, f32[576,384]{1,0:T(8,128)}, ...) | async-done | bytes 4718608 | tf_op jit(solution)/shard_map/psum | solution.py:380
  (298 shorter events, 289.5 us)
Async XLA Ops:
  7.2 516.6 %copy-start = (bf16[384,768]{1,0:T(8,128)(2,1)S(1)}, bf16[384,768]{1,0:T(8,128)(2,1)}, u32[]{:S(2)}) copy-start(bf16[384,768]{1,0:T(8,128)(2,1)} %param.28) | copy-start | bytes 1769476
  7.2 64.0 %all-gather.10.cloned.1.call-start = ((), (), s32[]{:S(2)}) async-start(), calls=%async_computation.9 | async-start | bytes 2949120 | tf_op jit(solution)/shard_map/all_gather | solution.py:56
  19.3 143.2 %reduce-scatter.10.cloned.1.call-start = ((), (), s32[]{:S(2)}) async-start(), calls=%async_computation.10 | async-start | bytes 10616832 | tf_op jit(solution)/shard_map/reduce_scatter | solution.py:65
  77.9 125.5 %all-gather.12.cloned.1.call-start = ((), (), s32[]{:S(2)}) async-start(), calls=%async_computation.11 | async-start | bytes 3538944 | tf_op jit(solution)/shard_map/all_gather | solution.py:261
  79.3 86.3 %copy-start.20 = (f32[1536,32]{0,1:T(8,128)}, f32[1536,32]{0,1:T(8,128)S(1)}, u32[]{:S(2)}) copy-start(f32[1536,32]{0,1:T(8,128)S(1)} %get-tuple-element.356) | copy-start | bytes 589828
  79.3 86.3 %copy-start.22 = (f32[1536,32]{0,1:T(8,128)}, f32[1536,32]{0,1:T(8,128)S(1)}, u32[]{:S(2)}) copy-start(f32[1536,32]{0,1:T(8,128)S(1)} %get-tuple-element.357) | copy-start | bytes 589828
  167.2 163.3 %all-gather.14.cloned.1.call-start = ((), (), s32[]{:S(2)}) async-start(), calls=%async_computation.12 | async-start | bytes 1769472 | tf_op jit(solution)/shard_map/all_gather | solution.py:76
  307.5 112.8 %reduce-scatter.12.cloned.1.call-start = ((), (), s32[]{:S(2)}) async-start(), calls=%async_computation.13 | async-start | bytes 5898240 | tf_op jit(solution)/shard_map/reduce_scatter | solution.py:85
  334.9 85.4 %copy-start.7 = (bf16[768,384]{1,0:T(8,128)(2,1)S(1)}, bf16[768,384]{1,0:T(8,128)(2,1)}, u32[]{:S(2)}) copy-start(bf16[768,384]{1,0:T(8,128)(2,1)} %param.18) | copy-start | bytes 1769476
  334.9 85.4 %copy-start.42 = (f32[384]{0:T(512)S(1)}, f32[384]{0:T(512)}, u32[]{:S(2)}) copy-start(f32[384]{0:T(512)} %get-tuple-element.258) | copy-start | bytes 4612
  334.9 138.0 %all-gather.20.cloned.1.call-start = ((), (), s32[]{:S(2)}) async-start(), calls=%async_computation.18 | async-start | bytes 2949120 | tf_op jit(solution)/shard_map/all_gather | solution.py:56
  337.5 186.3 %all-gather.16.cloned.1.call-start = ((), (), s32[]{:S(2)}) async-start(), calls=%async_computation.14 | async-start | bytes 2949120 | tf_op jit(solution)/shard_map/all_gather | solution.py:56
  428.1 207.4 %reduce-scatter.18.cloned.1.call-start = ((), (), s32[]{:S(2)}) async-start(), calls=%async_computation.19 | async-start | bytes 14155776 | tf_op jit(solution)/shard_map/reduce_scatter | solution.py:65
  480.8 267.7 %reduce-scatter.14.cloned.1.call-start = ((), (), s32[]{:S(2)}) async-start(), calls=%async_computation.15 | async-start | bytes 14155776 | tf_op jit(solution)/shard_map/reduce_scatter | solution.py:65
  532.0 287.7 %all-gather.22.cloned.1.call-start = ((), (), s32[]{:S(2)}) async-start(), calls=%async_computation.20 | async-start | bytes 7077888 | tf_op jit(solution)/shard_map/all_gather | solution.py:76
  756.9 127.0 %all-gather.18.cloned.1.call-start = ((), (), s32[]{:S(2)}) async-start(), calls=%async_computation.16 | async-start | bytes 7077888 | tf_op jit(solution)/shard_map/all_gather | solution.py:76
  757.6 213.7 %reduce-scatter.20.cloned.1.call-start = ((), (), s32[]{:S(2)}) async-start(), calls=%async_computation.21 | async-start | bytes 5898240 | tf_op jit(solution)/shard_map/reduce_scatter | solution.py:85
  826.8 232.7 %reduce-scatter.16.cloned.1.call-start = ((), (), s32[]{:S(2)}) async-start(), calls=%async_computation.17 | async-start | bytes 5898240 | tf_op jit(solution)/shard_map/reduce_scatter | solution.py:85
  891.0 80.4 %copy-start.46 = (f32[384]{0:T(512)S(1)}, f32[384]{0:T(512)}, u32[]{:S(2)}) copy-start(f32[384]{0:T(512)} %param.27) | copy-start | bytes 4612
  891.0 168.5 %copy-start.15 = (f32[768,384]{1,0:T(8,128)S(1)}, f32[768,384]{1,0:T(8,128)}, u32[]{:S(2)}) copy-start(f32[768,384]{1,0:T(8,128)} %reduce-scatter.12.cloned.1.call-done) | copy-start | bytes 3538948
  891.0 168.5 %copy-start.44 = (f32[384]{0:T(512)S(1)}, f32[384]{0:T(512)}, u32[]{:S(2)}) copy-start(f32[384]{0:T(512)} %get-tuple-element.253) | copy-start | bytes 4612
  891.0 168.5 %copy-start.61 = (f32[384]{0:T(512)S(1)}, f32[384]{0:T(512)}, u32[]{:S(2)}) copy-start(f32[384]{0:T(512)} %param.31) | copy-start | bytes 4612
  891.0 224.6 %all-gather.24.cloned.1.call-start = ((), (), s32[]{:S(2)}) async-start(), calls=%async_computation.22 | async-start | bytes 2949120 | tf_op jit(solution)/shard_map/all_gather | solution.py:56
  1064.9 88.5 %reduce-scatter.22.cloned.1.call-start = ((), (), s32[]{:S(2)}) async-start(), calls=%async_computation.23 | async-start | bytes 3538944 | tf_op jit(solution)/shard_map/reduce_scatter | solution.py:65
  1119.7 221.8 %reduce-scatter.24.cloned.1.call-start = ((), (), s32[]{:S(2)}) async-start(), calls=%async_computation.24 | async-start | bytes 3538944 | tf_op jit(solution)/shard_map/reduce_scatter | solution.py:298
  1306.5 88.5 %all-gather.26.cloned.1.call-start = ((), (), s32[]{:S(2)}) async-start(), calls=%async_computation.25 | async-start | bytes 5308416 | tf_op jit(solution)/shard_map/all_gather | solution.py:76
  1345.5 141.6 %reduce-scatter.26.cloned.1.call-start = ((), (), s32[]{:S(2)}) async-start(), calls=%async_computation.26 | async-start | bytes 5898240 | tf_op jit(solution)/shard_map/reduce_scatter | solution.py:85
  1401.6 218.0 %all-reduce.13.cloned.1.call-start = ((), (), s32[]{:S(2)}) async-start(), calls=%async_computation.27 | async-start | bytes 9437184 | tf_op jit(solution)/shard_map/psum | solution.py:380
  1416.8 70.3 %copy-start.36 = (f32[768]{0:T(1024)S(1)}, f32[768]{0:T(1024)}, u32[]{:S(2)}) copy-start(f32[768]{0:T(1024)} %copy-done.35) | copy-start | bytes 9220
  1416.8 70.3 %copy-start.38 = (f32[384]{0:T(512)S(1)}, f32[384]{0:T(512)}, u32[]{:S(2)}) copy-start(f32[384]{0:T(512)} %copy-done.37) | copy-start | bytes 4612
  1416.8 70.3 %copy-start.41 = (f32[384]{0:T(512)S(1)}, f32[384]{0:T(512)}, u32[]{:S(2)}) copy-start(f32[384]{0:T(512)} %param.24) | copy-start | bytes 4612
  1419.7 107.0 %copy-start.60 = (f32[128]{0:T(128)S(1)}, f32[128]{0:T(128)}, u32[]{:S(2)}) copy-start(f32[128]{0:T(128)} %copy-done.59) | copy-start | bytes 1540
  (54 other events, 659.3 us)
Sparse Core Ops, SparseCore 0:
  19.4 51.7 all-gather.9
  78.0 84.4 reduce-scatter.9
  167.3 36.0 all-gather.11
  307.6 22.7 all-gather.13
  335.0 85.2 reduce-scatter.11
  422.3 50.5 all-gather.19
  475.0 48.7 all-gather.15
  526.1 109.3 reduce-scatter.17
  637.8 110.6 reduce-scatter.13
  757.0 62.6 all-gather.21
  821.2 62.6 all-gather.17
  886.0 85.2 reduce-scatter.19
  973.6 85.7 reduce-scatter.15
  1065.0 50.5 all-gather.23
  1119.8 33.5 reduce-scatter.21
  1306.6 34.7 reduce-scatter.23
  1345.6 49.3 all-gather.25
  1401.7 85.2 reduce-scatter.25
  1528.0 91.4 all-reduce.12
where the time goes:
time: 1640 us; the launch traced here: 1630 us
  waiting for transfers between devices  1160 us (71%)
  matrix products  238 us (15%)
  other arithmetic  106 us (6%)
  blocking collectives  70.1 us (4%)
  local copies, waits for them, and re-layouts  38.3 us (2%)
    reduce_scatter x4, waiting for transfers between devices, into_heads(): lax.psum_scatter(partial_product(jnp.int32(0), share_rows * lax.axis_size...  333 us
    reduce_scatter x4, waiting for transfers between devices, into_stream(): lax.psum_scatter(partial_product(jnp.int32(0), share_rows * lax.axis_size...  311 us
    all_gather x4, waiting for transfers between devices, into_stream(): gathered = lax.all_gather(activation, 'row', axis=0, tiled=True)  191 us
    all_gather x4, waiting for transfers between devices, into_heads(): gathered = lax.all_gather(activation, 'col', axis=0, tiled=True)  190 us
    psum x1, waiting for transfers between devices, shards(): lax.psum((d_qkv, d_out_proj, d_up, d_down, d_mod_w, small_rows, d_up_bias...  72 us
    dot_general x8, matrix products, partial_product(): lax.dot_general(gathered, weight, (((1,), (contract,)), ((), ())), prefer...  52 us
    dot_general x10, matrix products, weight_grad(): lax.dot_general(first_operand, second_operand, (((0,), (0,)), ((), ())),...  43 us
    dot_general x3, matrix products, attend_back(): lax.dot_general(query_head, key_head, (((1,), (1,)), ((), ())), preferred...  40.2 us
  transfers between devices with their start and end apart: 19, of which 19 were waited for; matrix products, arithmetic and copies ran while one was open for 4% of the time, Pallas kernels for 0%

commit v1 on v0

--- a/solution.py
+++ b/solution.py
@@ -11,6 +11,12 @@
 PIECES = 4
 precise = lax.Precision.HIGHEST
 epsilon = 1e-05
+
+
+def in_order(pieces, dim):
+    lengths = list(pieces.shape[1:])
+    lengths[dim] *= pieces.shape[0]
+    return jnp.moveaxis(pieces, 0, dim).reshape(lengths)
 
 
 def embed_time(time_step):
@@ -53,7 +59,19 @@
 
 
 def into_heads(activation, weight, contract):
-    gathered = lax.all_gather(activation, "col", axis=0, tiled=True)
+    length = lax.axis_size("col")
+    pairs = [(i, (i + 1) % length) for i in range(length)]
+    back = [(b, a) for a, b in pairs]
+    lower, upper = ([], [])
+    for lap in range(length - 1):
+        if lap % 2 == 0:
+            lower.append(lax.ppermute(lower[-1] if lower else activation, "col", pairs))
+        else:
+            upper.append(lax.ppermute(upper[-1] if upper else activation, "col", back))
+    tiles = jnp.stack([*lower[::-1], activation, *upper])
+    shift = lax.axis_index("col") - len(lower)
+    tiles = tiles[(jnp.arange(length) - shift) % length]
+    gathered = in_order(tiles, 0)
     share_rows = gathered.shape[0] // lax.axis_size("row")
 
     def partial_product(start_row, row_count):

time: 1640 us -> 1560 us (0.951)
  waiting for transfers between devices: 1160 us -> 1020 us
  starting transfers between devices: 1.75 us -> 55 us
    all_gather x4 -> x0, waiting for transfers between devices: 190 us -> none  [into_heads(): gathered = lax.all_gather(activation, 'col', axis=0, tiled=True)]
    ppermute x0 -> x12, waiting for transfers between devices: none -> 146 us  [the longest x8 123 us: into_heads(): lower.append(lax.ppermute(lower[-1] if lower else activation, 'col', pairs))]
    ppermute x0 -> x12, starting transfers between devices: none -> 53.8 us  [the longest x8 44.3 us: into_heads(): lower.append(lax.ppermute(lower[-1] if lower else activation, 'col', pairs))]
    reduce_scatter x4, waiting for transfers between devices: 311 us -> 258 us  [into_stream(): lax.psum_scatter(partial_product(jnp.int32(0), share_rows * lax.axis_size...]
    reduce_scatter x4, waiting for transfers between devices: 333 us -> 283 us  [into_heads(): lax.psum_scatter(partial_product(jnp.int32(0), share_rows * lax.axis_size...]
  transfers between devices with their start and end apart: 19 -> 27, of which waited for: 19 -> 27; matrix products, arithmetic and copies ran while one was open for 4% -> 4% of each run, Pallas kernels for 0% -> 0%
where the time goes in v1:
time: 1560 us; the launch traced here: 1550 us
  waiting for transfers between devices  1020 us (65%)
  matrix products  230 us (15%)
  other arithmetic  115 us (7%)
  blocking collectives  70.1 us (4%)
  starting transfers between devices  55 us (4%)
  local copies, waits for them, and re-layouts  46.8 us (3%)
  between operations  15.8 us (1%)
    reduce_scatter x4, waiting for transfers between devices, into_heads(): lax.psum_scatter(partial_product(jnp.int32(0), share_rows * lax.axis_size...  283 us
    reduce_scatter x4, waiting for transfers between devices, into_stream(): lax.psum_scatter(partial_product(jnp.int32(0), share_rows * lax.axis_size...  258 us
    all_gather x4, waiting for transfers between devices, into_stream(): gathered = lax.all_gather(activation, 'row', axis=0, tiled=True)  191 us
    ppermute x8, waiting for transfers between devices, into_heads(): lower.append(lax.ppermute(lower[-1] if lower else activation, 'col', pairs))  123 us
    psum x1, waiting for transfers between devices, shards(): lax.psum((d_qkv, d_out_proj, d_up, d_down, d_mod_w, small_rows, d_up_bias...  72 us
    ppermute x8, starting transfers between devices, into_heads(): lower.append(lax.ppermute(lower[-1] if lower else activation, 'col', pairs))  44.3 us
    dot_general x8, matrix products, partial_product(): lax.dot_general(gathered, weight, (((1,), (contract,)), ((), ())), prefer...  44.3 us
    dot_general x10, matrix products, weight_grad(): lax.dot_general(first_operand, second_operand, (((0,), (0,)), ((), ())),...  42.9 us
  transfers between devices with their start and end apart: 27, of which 27 were waited for; matrix products, arithmetic and copies ran while one was open for 4% of the time, Pallas kernels for 0%

profile of v1, /device:TPU:0, one launch (start us, length us, event | category | flops | bytes accessed | tf_op | source)
XLA Modules:
  0.0 1550.5 jit_solution(10703771951746267699)
XLA Ops:
  24.4 14.1 collective-permute-done
  73.0 83.7 %reduce-scatter.10.cloned.1.call-done = f32[1536,576]{0,1:T(8,128)} async-done(((f32[3072,576]{0,1:T(8,128)}), f32[1536,576]{0,1:T(8,128)}) %reduce-scatter.10.cloned.1.call-update) | async-done | bytes 3538960 | tf_op jit(solution)/shard_map/reduce_scatter | solution.py:83
  165.8 31.8 %all-gather.6.cloned.1.call-done = bf16[3072,384]{0,1:T(8,128)(2,1)} async-done(((bf16[1536,384]{0,1:T(8,128)(2,1)}), bf16[3072,384]{0,1:T(8,128)(2,1)}) %all-gather.6.cloned.1.call-update) | async-done | bytes 2359312 | tf_op jit(solution)/shard_map/all_gather | solution.py:279
  207.4 93.6 %while.30 = (s32[]{:T(128)}, bf16[3,1536,64]{1,2,0:T(8,128)(2,1)S(1)}, f32[3,1536]{1,0:T(4,128)}, bf16[3,1536,64]{2,1,0:T(8,128)(2,1)}, bf16[3,3072,64]{2,1,0:T(...) while((s32[]{:T(128)}, ...), condition=%wide.region_10.11_spmd.clone.clone, body=%wide.region_7.10_spmd.clone.sunk.clone | while | flops 1264581120 | bytes 59093104 | solution.py:189
  207.4 12.4 fusion.170
  301.9 22.9 %all-gather.8.cloned.1.call-done = bf16[3072,192]{0,1:T(8,128)(2,1)} async-done(((bf16[1536,192]{0,1:T(8,128)(2,1)}), bf16[3072,192]{0,1:T(8,128)(2,1)}) %all-gather.8.cloned.1.call-update) | async-done | bytes 1179664 | tf_op jit(solution)/shard_map/all_gather | solution.py:94
  334.9 24.0 %collective-permute-done.6 = bf16[768,384]{1,0:T(8,128)(2,1)S(1)} collective-permute-done((bf16[768,384]{1,0:T(8,128)(2,1)S(1)}, bf16[768,384]{1,0:T(8,128)(2,1)S(1)}, u32[]{:S(2)}, u32[]{:S(2)}) %collective-permute-start.6) | collective-permute-done | bytes 589856 | tf_op jit(solution)/shard_map/ppermute | solution.py:68
  358.9 19.1 %collective-permute-start.7 = (bf16[768,384]{1,0:T(8,128)(2,1)S(1)}, bf16[768,384]{1,0:T(8,128)(2,1)S(1)}, u32[]{:S(2)}, u32[]{:S(2)}) collective-permute-start(bf16[768,384]{1,0:T(8,128)(2,1)S(1)} %collective-permute-done.6), channel_id=1, source_target_pairs={{0,1},{1,2},{2,3},{3,0},{4,5},{5,6},{6,7},{7,4},{8,9},{9,10},{10,1... | collective-permute-start | bytes 1769480 | tf_op jit(solution)/shard_map/ppermute | solution.py:68
  388.6 19.6 %collective-permute-done.7 = bf16[768,384]{1,0:T(8,128)(2,1)S(1)} collective-permute-done((bf16[768,384]{1,0:T(8,128)(2,1)S(1)}, bf16[768,384]{1,0:T(8,128)(2,1)S(1)}, u32[]{:S(2)}, u32[]{:S(2)}) %collective-permute-start.7) | collective-permute-done | bytes 589856 | tf_op jit(solution)/shard_map/ppermute | solution.py:68
  419.5 30.3 %reduce-scatter.12.cloned.1.call-done = f32[768,384]{1,0:T(8,128)} async-done(((f32[3072,384]{1,0:T(8,128)}), f32[768,384]{1,0:T(8,128)}) %reduce-scatter.12.cloned.1.call-update) | async-done | bytes 1179664 | tf_op jit(solution)/shard_map/reduce_scatter | solution.py:103
  460.6 14.2 collective-permute-done.3
  485.6 12.5 collective-permute-done.4
  508.6 53.0 %reduce-scatter.18.cloned.1.call-done = f32[1536,768]{1,0:T(8,128)} async-done(((f32[3072,768]{1,0:T(8,128)}), f32[1536,768]{1,0:T(8,128)}) %reduce-scatter.18.cloned.1.call-update) | async-done | bytes 4718608 | tf_op jit(solution)/shard_map/reduce_scatter | solution.py:83
  561.6 112.8 %reduce-scatter.14.cloned.1.call-done = f32[1536,768]{1,0:T(8,128)} async-done(((f32[3072,768]{1,0:T(8,128)}), f32[1536,768]{1,0:T(8,128)}) %reduce-scatter.14.cloned.1.call-update) | async-done | bytes 4718608 | tf_op jit(solution)/shard_map/reduce_scatter | solution.py:83
  683.6 62.0 %all-gather.12.cloned.1.call-done = bf16[3072,768]{1,0:T(8,128)(2,1)} async-done(((bf16[1536,768]{1,0:T(8,128)(2,1)}), bf16[3072,768]{1,0:T(8,128)(2,1)}) %all-gather.12.cloned.1.call-update) | async-done | bytes 4718608 | tf_op jit(solution)/shard_map/all_gather | solution.py:94
  753.0 56.8 %all-gather.10.cloned.1.call-done = bf16[3072,768]{1,0:T(8,128)(2,1)} async-done(((bf16[1536,768]{1,0:T(8,128)(2,1)}), bf16[3072,768]{1,0:T(8,128)(2,1)}) %all-gather.10.cloned.1.call-update) | async-done | bytes 4718608 | tf_op jit(solution)/shard_map/all_gather | solution.py:94
  817.1 80.4 %reduce-scatter.20.cloned.1.call-done = f32[768,384]{1,0:T(8,128)} async-done(((f32[3072,384]{1,0:T(8,128)}), f32[768,384]{1,0:T(8,128)}) %reduce-scatter.20.cloned.1.call-update) | async-done | bytes 1179664 | tf_op jit(solution)/shard_map/reduce_scatter | solution.py:103
  905.0 80.4 %reduce-scatter.16.cloned.1.call-done = f32[768,384]{1,0:T(8,128)} async-done(((f32[3072,384]{1,0:T(8,128)}), f32[768,384]{1,0:T(8,128)}) %reduce-scatter.16.cloned.1.call-update) | async-done | bytes 1179664 | tf_op jit(solution)/shard_map/reduce_scatter | solution.py:103
  992.9 14.2 collective-permute-done.9
  1038.4 34.0 %reduce-scatter.22.cloned.1.call-done = f32[1536,192]{0,1:T(8,128)} async-done(((f32[3072,192]{0,1:T(8,128)}), f32[1536,192]{0,1:T(8,128)}) %reduce-scatter.22.cloned.1.call-update) | async-done | bytes 1179664 | tf_op jit(solution)/shard_map/reduce_scatter | solution.py:83
  1074.5 147.2 %while.31 = (s32[]{:T(128)}, f32[3,1536,64]{1,2,0:T(8,128)}, bf16[3,3072,64]{1,2,0:T(8,128)(2,1)}, bf16[3,3072,64]{1,2,0:T(8,128)(2,1)}, bf16[3,1536,64]{2,1,0:T...) while((s32[]{:T(128)}, f32[3,1536,64]{1,2,0:T(8,128)}, ...), condition=%wide.region_27.28_spmd.clone.clone, body=%wide.region_25.27_spmd.clone.sunk.clone | while | flops 3081533952 | bytes 189987504 | solution.py:209
  1084.4 13.4 multiply_reduce_fusion.10
  1097.8 13.0 multiply_convert_fusion.5
  1133.5 13.4 multiply_reduce_fusion.10
  1146.9 13.0 multiply_convert_fusion.5
  1182.5 13.4 multiply_reduce_fusion.10
  1195.9 13.0 multiply_convert_fusion.5
  1225.1 34.9 %reduce-scatter.24.cloned.1.call-done = bf16[1536,384]{0,1:T(8,128)(2,1)} async-done(((bf16[3072,384]{0,1:T(8,128)(2,1)}), bf16[1536,384]{0,1:T(8,128)(2,1)}) %reduce-scatter.24.cloned.1.call-update) | async-done | bytes 1179664 | tf_op jit(solution)/shard_map/reduce_scatter | solution.py:316
  1263.7 49.2 %all-gather.14.cloned.1.call-done = bf16[3072,576]{0,1:T(8,128)(2,1)} async-done(((bf16[1536,576]{0,1:T(8,128)(2,1)}), bf16[3072,576]{0,1:T(8,128)(2,1)}) %all-gather.14.cloned.1.call-update) | async-done | bytes 3538960 | tf_op jit(solution)/shard_map/all_gather | solution.py:94
  1337.7 67.3 %reduce-scatter.26.cloned.1.call-done = f32[768,384]{1,0:T(8,128)} async-done(((f32[3072,384]{1,0:T(8,128)}), f32[768,384]{1,0:T(8,128)}) %reduce-scatter.26.cloned.1.call-update) | async-done | bytes 1179664 | tf_op jit(solution)/shard_map/reduce_scatter | solution.py:103
  1407.3 37.4 %all-reduce.4 = (f32[2,9,384]{2,1,0:T(8,128)S(1)}, f32[4,768]{1,0:T(4,128)S(1)}) all-reduce(f32[2,9,384]{2,1,0:T(8,128)S(1)} %broadcast_select_fusion, f32[4,768]{1,0:T(4,128)S(1)} %broadcast_select_fusion.1), channel_id=1, replica_groups=mesh['dp'=4,'row'=2,'col'=4] {'row','col'}, use_global_device_ids=true, to_apply=%region_43.44 | all-reduce | flops 9984 | bytes 79872 | tf_op jit(solution)/shard_map/psum | solution.py:355
  1465.5 72.0 %all-reduce.13.cloned.1.call-done = (f32[128,6,384]{2,0,1:T(8,128)}, f32[576,384]{1,0:T(8,128)}, f32[192,384]{1,0:T(8,128)}, f32[384,768]{1,0:T(8,128)}, f32[768,384]{1,0:T(8,128)}) async-done(((f32[128,6,384]{2,0,1:T(8,128)}, f32[576,384]{1,0:T(8,128)}, f32[192,384]{1,0:T(8,128)}, f32[384,768]{1,0:T(8,128)}, f32[768,384]{1,0:T(8,128)}), (f32[128,6,384]{2,0,1:T(8,128)}, f32[576,384]{1,0:T(8,128)}, ...) | async-done | bytes 4718608 | tf_op jit(solution)/shard_map/psum | solution.py:398
  (335 shorter events, 416.2 us)
Async XLA Ops:
  7.2 495.7 %copy-start = (bf16[384,768]{1,0:T(8,128)(2,1)S(1)}, bf16[384,768]{1,0:T(8,128)(2,1)}, u32[]{:S(2)}) copy-start(bf16[384,768]{1,0:T(8,128)(2,1)} %param.28) | copy-start | bytes 1769476
  7.2 149.5 %reduce-scatter.10.cloned.1.call-start = ((), (), s32[]{:S(2)}) async-start(), calls=%async_computation.9 | async-start | bytes 10616832 | tf_op jit(solution)/shard_map/reduce_scatter | solution.py:83
  20.2 18.4 %collective-permute-start = (bf16[768,384]{1,0:T(8,128)(2,1)S(1)}, bf16[768,384]{1,0:T(8,128)(2,1)S(1)}, u32[]{:S(2)}, u32[]{:S(2)}) collective-permute-start(bf16[768,384]{1,0:T(8,128)(2,1)S(1)} %fusion.66), channel_id=1, source_target_pairs={{0,1},{1,2},{2,3},{3,0},{4,5},{5,6},{6,7},{7,4},{8,9},{9,10},{10,1... | collective-permute-start | bytes 1769480 | tf_op jit(solution)/shard_map/ppermute | solution.py:68
  22.3 27.7 %collective-permute-start.2 = (bf16[768,384]{1,0:T(8,128)(2,1)S(1)}, bf16[768,384]{1,0:T(8,128)(2,1)S(1)}, u32[]{:S(2)}, u32[]{:S(2)}) collective-permute-start(bf16[768,384]{1,0:T(8,128)(2,1)S(1)} %fusion.66), channel_id=1, source_target_pairs={{1,0},{2,1},{3,2},{0,3},{5,4},{6,5},{7,6},{4,7},{9,8},{10,9},{11,1... | collective-permute-start | bytes 1769480 | tf_op jit(solution)/shard_map/ppermute | solution.py:70
  38.6 23.3 %collective-permute-start.1 = (bf16[768,384]{1,0:T(8,128)(2,1)S(1)}, bf16[768,384]{1,0:T(8,128)(2,1)S(1)}, u32[]{:S(2)}, u32[]{:S(2)}) collective-permute-start(bf16[768,384]{1,0:T(8,128)(2,1)S(1)} %collective-permute-done), channel_id=1, source_target_pairs={{0,1},{1,2},{2,3},{3,0},{4,5},{5,6},{6,7},{7,4},{8,9},{9,10},{10,1... | collective-permute-start | bytes 1769480 | tf_op jit(solution)/shard_map/ppermute | solution.py:68
  71.5 126.1 %all-gather.6.cloned.1.call-start = ((), (), s32[]{:S(2)}) async-start(), calls=%async_computation.10 | async-start | bytes 3538944 | tf_op jit(solution)/shard_map/all_gather | solution.py:279
  161.4 163.3 %all-gather.8.cloned.1.call-start = ((), (), s32[]{:S(2)}) async-start(), calls=%async_computation.11 | async-start | bytes 1769472 | tf_op jit(solution)/shard_map/all_gather | solution.py:94
  301.8 148.0 %reduce-scatter.12.cloned.1.call-start = ((), (), s32[]{:S(2)}) async-start(), calls=%async_computation.12 | async-start | bytes 5898240 | tf_op jit(solution)/shard_map/reduce_scatter | solution.py:103
  329.3 232.3 %reduce-scatter.18.cloned.1.call-start = ((), (), s32[]{:S(2)}) async-start(), calls=%async_computation.16 | async-start | bytes 14155776 | tf_op jit(solution)/shard_map/reduce_scatter | solution.py:83
  331.1 27.9 %collective-permute-start.6 = (bf16[768,384]{1,0:T(8,128)(2,1)S(1)}, bf16[768,384]{1,0:T(8,128)(2,1)S(1)}, u32[]{:S(2)}, u32[]{:S(2)}) collective-permute-start(bf16[768,384]{1,0:T(8,128)(2,1)S(1)} %get-tuple-element.325), channel_id=1, source_target_pairs={{0,1},{1,2},{2,3},{3,0},{4,5},{5,6},{6,7},{7,4},{8,9},{9,10},{10,1... | collective-permute-start | bytes 1769480 | tf_op jit(solution)/shard_map/ppermute | solution.py:68
  332.6 56.0 %collective-permute-start.8 = (bf16[768,384]{1,0:T(8,128)(2,1)S(1)}, bf16[768,384]{1,0:T(8,128)(2,1)S(1)}, u32[]{:S(2)}, u32[]{:S(2)}) collective-permute-start(bf16[768,384]{1,0:T(8,128)(2,1)S(1)} %get-tuple-element.325), channel_id=1, source_target_pairs={{1,0},{2,1},{3,2},{0,3},{5,4},{6,5},{7,6},{4,7},{9,8},{10,9},{11,1... | collective-permute-start | bytes 1769480 | tf_op jit(solution)/shard_map/ppermute | solution.py:70
  358.9 49.3 %collective-permute-start.7 = (bf16[768,384]{1,0:T(8,128)(2,1)S(1)}, bf16[768,384]{1,0:T(8,128)(2,1)S(1)}, u32[]{:S(2)}, u32[]{:S(2)}) collective-permute-start(bf16[768,384]{1,0:T(8,128)(2,1)S(1)} %collective-permute-done.6), channel_id=1, source_target_pairs={{0,1},{1,2},{2,3},{3,0},{4,5},{5,6},{6,7},{7,4},{8,9},{9,10},{10,1... | collective-permute-start | bytes 1769480 | tf_op jit(solution)/shard_map/ppermute | solution.py:68
  419.5 254.9 %reduce-scatter.14.cloned.1.call-start = ((), (), s32[]{:S(2)}) async-start(), calls=%async_computation.13 | async-start | bytes 14155776 | tf_op jit(solution)/shard_map/reduce_scatter | solution.py:83
  456.8 18.1 %collective-permute-start.3 = (bf16[768,384]{1,0:T(8,128)(2,1)S(1)}, bf16[768,384]{1,0:T(8,128)(2,1)S(1)}, u32[]{:S(2)}, u32[]{:S(2)}) collective-permute-start(bf16[768,384]{1,0:T(8,128)(2,1)S(1)} %add_convert_fusion.3), channel_id=1, source_target_pairs={{0,1},{1,2},{2,3},{3,0},{4,5},{5,6},{6,7},{7,4},{8,9},{9,10},{10,1... | collective-permute-start | bytes 1769480 | tf_op jit(solution)/shard_map/ppermute | solution.py:68
  458.0 27.6 %collective-permute-start.5 = (bf16[768,384]{1,0:T(8,128)(2,1)S(1)}, bf16[768,384]{1,0:T(8,128)(2,1)S(1)}, u32[]{:S(2)}, u32[]{:S(2)}) collective-permute-start(bf16[768,384]{1,0:T(8,128)(2,1)S(1)} %add_convert_fusion.3), channel_id=1, source_target_pairs={{1,0},{2,1},{3,2},{0,3},{5,4},{6,5},{7,6},{4,7},{9,8},{10,9},{11,1... | collective-permute-start | bytes 1769480 | tf_op jit(solution)/shard_map/ppermute | solution.py:70
  474.8 23.3 %collective-permute-start.4 = (bf16[768,384]{1,0:T(8,128)(2,1)S(1)}, bf16[768,384]{1,0:T(8,128)(2,1)S(1)}, u32[]{:S(2)}, u32[]{:S(2)}) collective-permute-start(bf16[768,384]{1,0:T(8,128)(2,1)S(1)} %collective-permute-done.3), channel_id=1, source_target_pairs={{0,1},{1,2},{2,3},{3,0},{4,5},{5,6},{6,7},{7,4},{8,9},{9,10},{10,1... | collective-permute-start | bytes 1769480 | tf_op jit(solution)/shard_map/ppermute | solution.py:68
  507.9 237.7 %all-gather.12.cloned.1.call-start = ((), (), s32[]{:S(2)}) async-start(), calls=%async_computation.17 | async-start | bytes 7077888 | tf_op jit(solution)/shard_map/all_gather | solution.py:94
  682.8 127.0 %all-gather.10.cloned.1.call-start = ((), (), s32[]{:S(2)}) async-start(), calls=%async_computation.14 | async-start | bytes 7077888 | tf_op jit(solution)/shard_map/all_gather | solution.py:94
  683.6 213.9 %reduce-scatter.20.cloned.1.call-start = ((), (), s32[]{:S(2)}) async-start(), calls=%async_computation.18 | async-start | bytes 5898240 | tf_op jit(solution)/shard_map/reduce_scatter | solution.py:103
  752.8 232.7 %reduce-scatter.16.cloned.1.call-start = ((), (), s32[]{:S(2)}) async-start(), calls=%async_computation.15 | async-start | bytes 5898240 | tf_op jit(solution)/shard_map/reduce_scatter | solution.py:103
  817.0 168.5 %copy-start.22 = (f32[768,384]{1,0:T(8,128)S(1)}, f32[768,384]{1,0:T(8,128)}, u32[]{:S(2)}) copy-start(f32[768,384]{1,0:T(8,128)} %reduce-scatter.12.cloned.1.call-done) | copy-start | bytes 3538948
  817.0 168.5 %copy-start.54 = (f32[384]{0:T(512)S(1)}, f32[384]{0:T(512)}, u32[]{:S(2)}) copy-start(f32[384]{0:T(512)} %get-tuple-element.253) | copy-start | bytes 4612
  817.0 168.5 %copy-start.67 = (f32[384]{0:T(512)S(1)}, f32[384]{0:T(512)}, u32[]{:S(2)}) copy-start(f32[384]{0:T(512)} %param.31) | copy-start | bytes 4612
  817.0 255.4 %reduce-scatter.22.cloned.1.call-start = ((), (), s32[]{:S(2)}) async-start(), calls=%async_computation.19 | async-start | bytes 3538944 | tf_op jit(solution)/shard_map/reduce_scatter | solution.py:83
  989.0 18.1 %collective-permute-start.9 = (bf16[768,384]{1,0:T(8,128)(2,1)S(1)}, bf16[768,384]{1,0:T(8,128)(2,1)S(1)}, u32[]{:S(2)}, u32[]{:S(2)}) collective-permute-start(bf16[768,384]{1,0:T(8,128)(2,1)S(1)} %multiply_convert_fusion.2), channel_id=1, source_target_pairs={{0,1},{1,2},{2,3},{3,0},{4,5},{5,6},{6,7},{7,4},{8,9},{9,10},{10,1... | collective-permute-start | bytes 1769480 | tf_op jit(solution)/shard_map/ppermute | solution.py:68
  990.6 28.5 %collective-permute-start.11 = (bf16[768,384]{1,0:T(8,128)(2,1)S(1)}, bf16[768,384]{1,0:T(8,128)(2,1)S(1)}, u32[]{:S(2)}, u32[]{:S(2)}) collective-permute-start(bf16[768,384]{1,0:T(8,128)(2,1)S(1)} %multiply_convert_fusion.2), channel_id=1, source_target_pairs={{1,0},{2,1},{3,2},{0,3},{5,4},{6,5},{7,6},{4,7},{9,8},{10,9},{11,1... | collective-permute-start | bytes 1769480 | tf_op jit(solution)/shard_map/ppermute | solution.py:70
  1007.1 24.1 %collective-permute-start.10 = (bf16[768,384]{1,0:T(8,128)(2,1)S(1)}, bf16[768,384]{1,0:T(8,128)(2,1)S(1)}, u32[]{:S(2)}, u32[]{:S(2)}) collective-permute-start(bf16[768,384]{1,0:T(8,128)(2,1)S(1)} %collective-permute-done.9), channel_id=1, source_target_pairs={{0,1},{1,2},{2,3},{3,0},{4,5},{5,6},{6,7},{7,4},{8,9},{9,10},{10,1... | collective-permute-start | bytes 1769480 | tf_op jit(solution)/shard_map/ppermute | solution.py:68
  1038.3 221.6 %reduce-scatter.24.cloned.1.call-start = ((), (), s32[]{:S(2)}) async-start(), calls=%async_computation.20 | async-start | bytes 3538944 | tf_op jit(solution)/shard_map/reduce_scatter | solution.py:316
  1225.0 87.9 %all-gather.14.cloned.1.call-start = ((), (), s32[]{:S(2)}) async-start(), calls=%async_computation.21 | async-start | bytes 5308416 | tf_op jit(solution)/shard_map/all_gather | solution.py:94
  1263.4 141.6 %reduce-scatter.26.cloned.1.call-start = ((), (), s32[]{:S(2)}) async-start(), calls=%async_computation.22 | async-start | bytes 5898240 | tf_op jit(solution)/shard_map/reduce_scatter | solution.py:103
  1319.6 218.0 %all-reduce.13.cloned.1.call-start = ((), (), s32[]{:S(2)}) async-start(), calls=%async_computation.23 | async-start | bytes 9437184 | tf_op jit(solution)/shard_map/psum | solution.py:398
  1337.7 107.0 %copy-start.66 = (f32[128]{0:T(128)S(1)}, f32[128]{0:T(128)}, u32[]{:S(2)}) copy-start(f32[128]{0:T(128)} %copy-done.65) | copy-start | bytes 1540
  (68 other events, 1643.8 us)
Sparse Core Ops, SparseCore 0:
  71.7 85.0 reduce-scatter.9
  161.5 36.0 all-gather.5
  301.9 22.7 all-gather.7
  329.4 120.3 reduce-scatter.11
  452.0 109.5 reduce-scatter.17
  563.7 110.6 reduce-scatter.13
  683.0 62.6 all-gather.11
  747.2 62.6 all-gather.9
  812.1 85.2 reduce-scatter.19
  899.6 85.7 reduce-scatter.15
  1038.4 33.8 reduce-scatter.21
  1225.1 34.7 reduce-scatter.23
  1263.6 49.3 all-gather.13
  1319.7 85.2 reduce-scatter.25
  1446.0 91.4 all-reduce.12
